TPU v7x, 32 devices: a whole 2x2x4 slice. The times are simulated.
32 devices in a mesh: row: 4 (over y, x), col: 8 (over z, core).
Axes of the slice: x: 2, y: 2, z: 4, core: 2. Of those that a mesh axis runs over, the one named last changes fastest.
Arguments:
- inv_sep: bfloat16 [24576, 24576], P('row', 'col'), may hold values from -6 to 6
- lower_one: bfloat16 [24576, 256], P('col', 'row'), may hold values from -0.078125 to 0.078125
- upper_one: bfloat16 [256, 24576], P('col', 'row'), may hold values from -0.078125 to 0.078125
- diag_inv_one: float32 [256, 256], replicated, may hold values from -6 to 6
- blocks_one: int32 [40], replicated, may hold values from 0 to 191, as said below
- lower_two: bfloat16 [24576, 256], P('col', 'row'), may hold values from -0.09375 to 0.09375
- upper_two: bfloat16 [256, 24576], P('col', 'row'), may hold values from -0.09375 to 0.09375
- corner_lower: bfloat16 [256, 256], replicated, may hold values from -0.375 to 0.375
- corner_upper: bfloat16 [256, 256], replicated, may hold values from -0.375 to 0.375
- diag_inv_two: float32 [256, 256], replicated, may hold values from -6 to 6
- blocks_two: int32 [32], replicated, may hold values from 0 to 191, as said below
Outputs:
- inv_lower_one: bfloat16 [5120, 256], P(('row', 'col'))
- inv_upper_one: bfloat16 [256, 5120], P('row', 'col')
- inv_diag_one: float32 [256, 256], replicated
- inv_lower_two: bfloat16 [4096, 256], P(('row', 'col'))
- inv_upper_two: bfloat16 [256, 4096], P('row', 'col')
- inv_diag_two: float32 [256, 256], replicated
Inputs may be any that keep to these rules, and one draw needn't show every extreme that they name: `blocks_one`: distinct block indices in increasing order; each aligned run of 24 blocks holds exactly 5 of them; the first and the last block of the separator are listed. `blocks_two`: distinct block indices in increasing order, each of them also in blocks_one; each aligned run of 24 blocks holds exactly 4 of them; the first and the last block of the separator are listed.
All inputs are finite; a program needn't handle non-finite values.
Results may differ from a plain program's by a relative error of at most 0.0039.
Values may be sent and summed in bfloat16 or wider, within the bound.
No kernel may reach another device: no remote copies, remote signals or barrier semaphores. Data moves between devices by JAX's collectives and lax.ppermute only.
A program may use at most 128 MiB of HBM per device.

v0:
```python
import jax
import jax.numpy as jnp
from jax import lax
from jax.sharding import PartitionSpec as P

B = 128


def highest(first_mat, second_mat):
    return jnp.dot(
        first_mat.astype(jnp.float32),
        second_mat.astype(jnp.float32),
        precision=lax.Precision.HIGHEST,
    )


def take_rows(matrix, blocks):
    shaped = matrix.reshape(matrix.shape[0] // B, B, matrix.shape[1])
    return jnp.take(shaped, blocks, axis=0).reshape(blocks.shape[0] * B, matrix.shape[1])


def take_cols(matrix, blocks):
    shaped = matrix.reshape(matrix.shape[0], matrix.shape[1] // B, B)
    return jnp.take(shaped, blocks, axis=1).reshape(matrix.shape[0], blocks.shape[0] * B)


def block_rows(blocks):
    return (blocks[:, None] * B + jnp.arange(B, dtype=jnp.int32)[None, :]).reshape(-1)


def places(wanted, listed):
    return jnp.sum((listed[None, :] < wanted[:, None]).astype(jnp.int32), axis=1)


def on_device(
    inv_sep,
    lower_one,
    upper_one,
    diag_inv_one,
    blocks_one,
    lower_two,
    upper_two,
    corner_lower,
    corner_upper,
    diag_inv_two,
    blocks_two,
):
    row_index = lax.axis_index("row")
    col_index = lax.axis_index("col")
    row_count = lax.axis_size("row")
    col_count = lax.axis_size("col")
    rows_here, cols_here = inv_sep.shape
    panel_width = diag_inv_one.shape[0]
    run_blocks = cols_here // B
    pick_one = blocks_one.shape[0] // col_count
    pick_two = blocks_two.shape[0] // col_count
    runs_group = col_count // row_count
    group_one = pick_one * runs_group
    group_two = pick_two * runs_group
    share_one = pick_one * B // row_count
    share_two = pick_two * B // row_count
    upper_rows = panel_width // row_count
    row_one = lax.dynamic_slice_in_dim(blocks_one, row_index * group_one, group_one) - row_index * (
        rows_here // B
    )
    row_two = lax.dynamic_slice_in_dim(blocks_two, row_index * group_two, group_two) - row_index * (
        rows_here // B
    )
    col_one = (
        lax.dynamic_slice_in_dim(blocks_one, col_index * pick_one, pick_one)
        - col_index * run_blocks
    )
    col_two = (
        lax.dynamic_slice_in_dim(blocks_two, col_index * pick_two, pick_two)
        - col_index * run_blocks
    )
    sep_one = take_cols(take_rows(inv_sep, row_one), col_one)
    sep_two = take_cols(take_rows(inv_sep, row_two), col_two)
    lower_spots = block_rows(places(row_two, row_one))
    upper_spots = places(col_two, col_one)
    corner_mine = lax.dynamic_slice_in_dim(corner_upper, row_index * upper_rows, upper_rows, 1)
    lower_p = lax.all_gather(take_rows(lower_one, col_one), "row", axis=1, tiled=True)
    upper_p = lax.all_gather(take_cols(upper_one, row_one), "col", axis=0, tiled=True)
    inv_lower_one = lax.psum_scatter(
        -jnp.dot(sep_one, lower_p, preferred_element_type=jnp.float32),
        "col",
        scatter_dimension=0,
        tiled=True,
    ).astype(jnp.bfloat16)
    inv_upper_one = lax.psum_scatter(
        -jnp.dot(upper_p, sep_one, preferred_element_type=jnp.float32),
        "row",
        scatter_dimension=0,
        tiled=True,
    ).astype(jnp.bfloat16)
    lower_c = lax.all_gather(take_rows(lower_two, col_two), "row", axis=1, tiled=True)
    upper_c = lax.all_gather(take_cols(upper_two, row_two), "col", axis=0, tiled=True)
    own_rows = col_index * share_one + jnp.arange(share_one, dtype=jnp.int32)
    chooser = (lower_spots[:, None] == own_rows[None, :]).astype(jnp.float32)
    carried = jnp.dot(inv_lower_one, corner_lower, preferred_element_type=jnp.float32)
    direct = jnp.dot(sep_two, lower_c, preferred_element_type=jnp.float32)
    shifted_part = jnp.dot(chooser, carried, precision=lax.Precision.HIGHEST)
    inv_lower_two = lax.psum_scatter(
        -(direct + shifted_part), "col", scatter_dimension=0, tiled=True
    ).astype(jnp.bfloat16)
    ancestor_cols = take_cols(inv_upper_one, upper_spots)
    direct = jnp.dot(upper_c, sep_two, preferred_element_type=jnp.float32)
    shifted_part = jnp.dot(corner_mine, ancestor_cols, preferred_element_type=jnp.float32)
    inv_upper_two = lax.psum_scatter(
        -(direct + shifted_part), "row", scatter_dimension=0, tiled=True
    ).astype(jnp.bfloat16)
    upper_slab = lax.dynamic_slice_in_dim(upper_p, col_index * share_one, share_one, 1)
    second_slab = lax.dynamic_slice_in_dim(upper_c, col_index * share_two, share_two, 1)
    first_part = jnp.dot(upper_slab, inv_lower_one, preferred_element_type=jnp.float32)
    cross = jnp.dot(ancestor_cols, lower_c, preferred_element_type=jnp.float32)
    second_part = jnp.dot(second_slab, inv_lower_two, preferred_element_type=jnp.float32) - highest(
        corner_mine, cross
    )
    extra_part = highest(corner_upper, highest(first_part, corner_lower))
    first_total, second_total = lax.psum((first_part, second_part + extra_part), ("row", "col"))
    inv_diag_one = diag_inv_one - first_total
    tail_term = highest(corner_upper, highest(diag_inv_one, corner_lower))
    inv_diag_two = diag_inv_two - (second_total - tail_term)
    return (inv_lower_one, inv_upper_one, inv_diag_one, inv_lower_two, inv_upper_two, inv_diag_two)


def solution(mesh):
    return jax.shard_map(
        on_device,
        mesh=mesh,
        in_specs=(
            P("row", "col"),
            P("col", "row"),
            P("col", "row"),
            P(),
            P(),
            P("col", "row"),
            P("col", "row"),
            P(),
            P(),
            P(),
            P(),
        ),
        out_specs=(
            P(("row", "col"), None),
            P("row", "col"),
            P(),
            P(("row", "col"), None),
            P("row", "col"),
            P(),
        ),
        check_vma=False,
    )
```

profile of v0, /device:TPU:0, one launch (start us, length us, event | category | flops | bytes accessed | tf_op | source)
XLA Modules:
  0.0 326.0 jit_solution(9898332100142515147)
XLA Ops:
  7.2 0.8 compare_and_fusion.3
  8.0 8.8 %gather_fusion = bf16[10,128,3072]{2,1,0:T(8,128)(2,1)} fusion(bf16[48,128,3072]{2,1,0:T(8,128)(2,1)} %bitcast.126, s32[1024]{0:T(1024)S(1)} %pad_clamp_fusion.4), kind=kCustom, calls=%fused_computation | custom fusion | bytes 15728680 | tf_op jit(solution)/shard_map/jit(_take)/gather | solution.py:19
  16.8 8.3 %copy.69 = bf16[160,8,24,128]{3,2,1,0:T(8,128)(2,1)} copy(bf16[160,8,24,128]{3,1,2,0:T(8,128)(2,1)} %bitcast.121) | data formatting | bytes 15728640
  25.2 8.6 %copy_select_fusion = bf16[1280,24,128]{2,0,1:T(8,128)(2,1)} fusion(bf16[1280,24,128]{2,1,0:T(8,128)(2,1)} %bitcast.122, pred[1280]{0:T(1024)(128)(4,1)S(1)} %broadcast_bitcast_fusion), kind=kLoop, calls=%fused_computation.9 | loop fusion | flops 3932160 | bytes 15729920 | tf_op jit(solution)/shard_map/jit(_take)/select_n | solution.py:19
  33.8 4.1 %gather_fusion.1 = bf16[5,1280,128]{2,1,0:T(8,128)(2,1)S(1)} fusion(bf16[1280,24,128]{2,0,1:T(8,128)(2,1)} %copy_select_fusion, s32[1024]{0:T(1024)S(1)} %pad_clamp_fusion.3), kind=kCustom, calls=%fused_computation.1 | custom fusion | bytes 3276820 | tf_op jit(solution)/shard_map/jit(_take)/gather | solution.py:24
  37.9 2.4 copy.42
  40.5 0.6 gather_fusion.2
  41.1 1.6 bitcast_select_fusion
  42.8 10.9 %all_gather.12 = bf16[640,256]{0,1:T(8,128)(2,1)S(1)} all-gather(bf16[640,64]{0,1:T(8,128)(2,1)S(1)} %bitcast_select_fusion.3), channel_id=1, replica_groups=mesh['row'=4,'col'=8] {'row'}, dimensions={1}, use_global_device_ids=true | all-gather | bytes 409600 | tf_op jit(solution)/shard_map/all_gather | solution.py:82
  53.7 1.8 convolution_negate_fusion
  55.6 0.6 gather_fusion.3
  56.2 17.9 %all_gather.13 = bf16[256,1280]{1,0:T(8,128)(2,1)S(1)} all-gather(bf16[32,1280]{1,0:T(8,128)(2,1)S(1)} %bitcast_select_fusion.2), channel_id=1, replica_groups=mesh['row'=4,'col'=8] {'col'}, dimensions={0}, use_global_device_ids=true | all-gather | bytes 737280 | tf_op jit(solution)/shard_map/all_gather | solution.py:83
  74.1 1.6 convolution_negate_fusion.1
  76.1 0.7 convert_reduce_fusion
  77.1 6.4 %gather_fusion.4 = bf16[8,128,3072]{2,1,0:T(8,128)(2,1)} fusion(bf16[48,128,3072]{2,1,0:T(8,128)(2,1)} %bitcast.127, s32[1024]{0:T(1024)S(1)} %pad_clamp_fusion.2), kind=kCustom, calls=%fused_computation.4 | custom fusion | bytes 12582944 | tf_op jit(solution)/shard_map/jit(_take)/gather | solution.py:19
  83.5 4.8 %copy.70 = bf16[128,8,24,128]{3,2,1,0:T(8,128)(2,1)S(1)} copy(bf16[128,8,24,128]{3,1,2,0:T(8,128)(2,1)} %bitcast.124) | data formatting | bytes 12582912
  88.4 4.2 %copy_select_fusion.1 = bf16[1024,24,128]{2,0,1:T(8,128)(2,1)} fusion(bf16[1024,24,128]{2,1,0:T(8,128)(2,1)S(1)} %bitcast.123, pred[1024]{0:T(1024)(128)(4,1)S(1)} %broadcast_bitcast_fusion.1), kind=kLoop, calls=%fused_computation.10 | loop fusion | flops 3145728 | bytes 12583936 | tf_op jit(solution)/shard_map/jit(_take)/select_n | solution.py:19
  92.6 3.6 %gather_fusion.5 = bf16[4,1024,128]{2,1,0:T(8,128)(2,1)S(1)} fusion(bf16[1024,24,128]{2,0,1:T(8,128)(2,1)} %copy_select_fusion.1, s32[1024]{0:T(1024)S(1)} %pad_clamp_fusion.1), kind=kCustom, calls=%fused_computation.5 | custom fusion | bytes 2097168 | tf_op jit(solution)/shard_map/jit(_take)/gather | solution.py:24
  96.2 0.5 copy.48
  96.8 1.1 copy_bitcast_fusion.1
  97.9 0.6 gather_fusion.6
  98.5 9.4 %all_gather.14 = bf16[512,256]{0,1:T(8,128)(2,1)S(1)} all-gather(bf16[512,64]{0,1:T(8,128)(2,1)S(1)} %bitcast_select_fusion.6), channel_id=1, replica_groups=mesh['row'=4,'col'=8] {'row'}, dimensions={1}, use_global_device_ids=true | all-gather | bytes 327680 | tf_op jit(solution)/shard_map/all_gather | solution.py:96
  107.9 0.7 broadcast_multiply_fusion
  108.6 1.8 copy_bitcast_fusion
  110.7 0.5 fusion.25
  111.2 0.9 convert_element_type.24
  112.3 1.6 fusion
  114.0 1.6 gather_fusion.7
  115.8 14.8 %all_gather.15 = bf16[256,1024]{1,0:T(8,128)(2,1)S(1)} all-gather(bf16[32,1024]{1,0:T(8,128)(2,1)S(1)} %bitcast_select_fusion.5), channel_id=1, replica_groups=mesh['row'=4,'col'=8] {'col'}, dimensions={0}, use_global_device_ids=true | all-gather | bytes 589824 | tf_op jit(solution)/shard_map/all_gather | solution.py:97
  130.6 0.9 copy_bitcast_fusion.4
  131.6 0.6 gather_fusion.8
  132.1 0.6 copy-done.6
  132.8 0.8 fusion.15
  133.6 1.2 fusion.13
  134.8 1.3 fusion.1
  136.1 1.1 fusion.8
  137.3 0.3 fusion.27
  137.6 16.6 %reduce-scatter.9.cloned.1.call-done = f32[128,256]{1,0:T(8,128)} async-done(((f32[1024,256]{1,0:T(8,128)}), f32[128,256]{1,0:T(8,128)}) %reduce-scatter.9.cloned.1.call-update) | async-done | bytes 131088 | tf_op jit(solution)/shard_map/reduce_scatter | solution.py:103
  154.1 0.9 convert_element_type.27
  155.2 1.2 convolution_subtract_fusion
  156.4 1.9 fusion.4
  158.4 1.2 fusion.28
  159.6 0.6 convert_element_type.25
  160.3 20.1 %reduce-scatter.11.cloned.1.call-done = f32[64,512]{1,0:T(8,128)} async-done(((f32[256,512]{1,0:T(8,128)}), f32[64,512]{1,0:T(8,128)}) %reduce-scatter.11.cloned.1.call-update) | async-done | bytes 131088 | tf_op jit(solution)/shard_map/reduce_scatter | solution.py:109
  180.3 1.5 convert_element_type.29
  181.9 133.7 %all-reduce.3.cloned.1.call-done = (f32[256,256]{1,0:T(8,128)}, f32[256,256]{1,0:T(8,128)}) async-done(((f32[256,256]{1,0:T(8,128)}, f32[256,256]{1,0:T(8,128)}), (f32[256,256]{1,0:T(8,128)}, f32[256,256]{1,0:T(8,128)})) %all-reduce.3.cloned.1.call-update) | async-done | bytes 524304 | tf_op jit(solution)/shard_map/psum | solution.py:120
  315.6 1.8 sub.40
  317.4 2.1 fusion.3
  (64 shorter events, 2.3 us)
Async XLA Ops:
  7.2 33.2 %copy-start = (bf16[3072,64]{0,1:T(8,128)(2,1)S(1)}, bf16[3072,64]{0,1:T(8,128)(2,1)}, u32[]{:S(2)}) copy-start(bf16[3072,64]{0,1:T(8,128)(2,1)} %param.12) | copy-start | bytes 1179652
  7.2 104.0 %reduce-scatter.5.cloned.1.call-start = ((), (), s32[]{:S(2)}) async-start(), calls=%async_computation.4 | async-start | bytes 1474560 | tf_op jit(solution)/shard_map/reduce_scatter | solution.py:84
  16.8 8.3 %copy-start.9 = (s32[40]{0:T(128)S(1)}, s32[40]{0:T(128)}, u32[]{:S(2)}) copy-start(s32[40]{0:T(128)} %param.15) | copy-start | bytes 484
  40.3 15.2 %copy-start.7 = (bf16[32,6144]{1,0:T(8,128)(2,1)S(1)}, bf16[32,6144]{1,0:T(8,128)(2,1)}, u32[]{:S(2)}) copy-start(bf16[32,6144]{1,0:T(8,128)(2,1)} %param.13) | copy-start | bytes 1179652
  53.7 22.3 %copy-start.10 = (s32[32]{0:T(128)S(1)}, s32[32]{0:T(128)}, u32[]{:S(2)}) copy-start(s32[32]{0:T(128)} %param.21) | copy-start | bytes 388
  55.5 75.1 %reduce-scatter.7.cloned.1.call-start = ((), (), s32[]{:S(2)}) async-start(), calls=%async_computation.5 | async-start | bytes 819200 | tf_op jit(solution)/shard_map/reduce_scatter | solution.py:90
  75.8 78.4 %reduce-scatter.9.cloned.1.call-start = ((), (), s32[]{:S(2)}) async-start(), calls=%async_computation.6 | async-start | bytes 1179648 | tf_op jit(solution)/shard_map/reduce_scatter | solution.py:103
  92.6 19.5 %copy-start.3 = (bf16[256,256]{1,0:T(8,128)(2,1)S(1)}, bf16[256,256]{1,0:T(8,128)(2,1)}, u32[]{:S(2)}) copy-start(bf16[256,256]{1,0:T(8,128)(2,1)} %param.18) | copy-start | bytes 393220
  112.1 1.8 copy-start.4
  114.0 205.5 %copy-start.1 = (bf16[3072,64]{0,1:T(8,128)(2,1)S(1)}, bf16[3072,64]{0,1:T(8,128)(2,1)}, u32[]{:S(2)}) copy-start(bf16[3072,64]{0,1:T(8,128)(2,1)} %param.12) | copy-start | bytes 1179652
  114.0 66.3 %reduce-scatter.11.cloned.1.call-start = ((), (), s32[]{:S(2)}) async-start(), calls=%async_computation.7 | async-start | bytes 655360 | tf_op jit(solution)/shard_map/reduce_scatter | solution.py:109
  132.1 0.6 copy-start.6
  133.6 26.0 %copy-start.5 = (f32[64,640]{1,0:T(8,128)S(1)}, f32[64,640]{1,0:T(8,128)}, u32[]{:S(2)}) copy-start(f32[64,640]{1,0:T(8,128)} %reduce-scatter.7.cloned.1.call-done) | copy-start | bytes 491524
  136.1 179.5 %all-reduce.3.cloned.1.call-start = ((), (), s32[]{:S(2)}) async-start(), calls=%async_computation.8 | async-start | bytes 1048576 | tf_op jit(solution)/shard_map/psum | solution.py:120
  137.3 21.1 %copy-start.2 = (f32[256,256]{1,0:T(8,128)}, f32[256,256]{1,0:T(8,128)S(1)}, u32[]{:S(2)}) copy-start(f32[256,256]{1,0:T(8,128)S(1)} %fusion.8) | copy-start | bytes 786436
  155.1 164.4 %copy-start.8 = (bf16[128,256]{1,0:T(8,128)(2,1)}, bf16[128,256]{1,0:T(8,128)(2,1)S(1)}, u32[]{:S(2)}) copy-start(bf16[128,256]{1,0:T(8,128)(2,1)S(1)} %convert_element_type.27) | copy-start | bytes 196612
Sparse Core Ops, SparseCore 0:
  55.6 34.0 reduce-scatter.4
  92.6 26.4 reduce-scatter.6
  121.4 32.6 reduce-scatter.8
  156.8 23.4 reduce-scatter.10
  186.2 129.3 all-reduce.2
where the time goes:
time: 327 us; the launch traced here: 326 us
  waiting for transfers between devices  170 us (52%)
  blocking collectives  53.1 us (16%)
  local copies, waits for them, and re-layouts  46.8 us (14%)
  other arithmetic  24.2 us (7%)
  matrix products  17 us (5%)
  between operations  14.1 us (4%)
    psum x1, waiting for transfers between devices, on_device(): lax.psum((first_part, second_part + extra_part), ('row', 'col'))  134 us
    reduce_scatter x1, waiting for transfers between devices, on_device(): lax.psum_scatter(-(direct + shifted_part), 'row', scatter_dimension=0, ti...  20.1 us
    all_gather x1, blocking collectives, on_device(): lax.all_gather(take_cols(upper_one, row_one), 'col', axis=0, tiled=True)  17.9 us
    reduce_scatter x1, waiting for transfers between devices, on_device(): lax.psum_scatter(-(direct + shifted_part), 'col', scatter_dimension=0, ti...  16.6 us
    gather x4, local copies, waits for them, and re-layouts, take_rows(): jnp.take(shaped, blocks, axis=0)  16.4 us
    all_gather x1, blocking collectives, on_device(): lax.all_gather(take_cols(upper_two, row_two), 'col', axis=0, tiled=True)  14.8 us
    unnamed x24, local copies, waits for them, and re-layouts  13.7 us
    gather x7, local copies, waits for them, and re-layouts, take_cols(): jnp.take(shaped, blocks, axis=1)  13.3 us
  transfers between devices with their start and end apart: 5, of which 3 were waited for; matrix products, arithmetic and copies ran while one was open for 14% of the time, Pallas kernels for 0%

commit v1 on v0

v1 whole, which is shorter than its diff:
```python
import jax
import jax.numpy as jnp
from jax import lax
from jax.experimental import pallas as pl
from jax.experimental.pallas import tpu as pltpu
from jax.sharding import PartitionSpec as P

B = 128
F32 = jnp.float32
BF16 = jnp.bfloat16

PAIR_TYPE = F32
Z_TYPE = BF16
ROW_TYPE = BF16
DIAG_PAIR = F32
DIAG_Z = BF16
DIAG_OUT = BF16

NT = (((1,), (1,)), ((), ()))
TN = (((0,), (0,)), ((), ()))


def dot(a, b):
    return jnp.dot(a, b, preferred_element_type=F32)


def split(x):
    high = x.astype(BF16)
    return high, (x - high.astype(F32)).astype(BF16)


def exchange(x, axis, size, distance):
    return lax.ppermute(x, axis, [(s, s ^ distance) for s in range(size)])


def in_hbm(x):
    return pltpu.with_memory_space_constraint(x, pltpu.HBM)


def shape(dims, dtype):
    return jax.ShapeDtypeStruct(dims, dtype)


VMEM = pl.BlockSpec(memory_space=pltpu.VMEM)
SMEM = pl.BlockSpec(memory_space=pltpu.SMEM)
HBM = pl.BlockSpec(memory_space=pltpu.HBM)


def call(body, in_specs, outs, scratch=(), mib=8):
    return pl.pallas_call(
        body,
        out_shape=tuple(outs),
        in_specs=in_specs,
        out_specs=tuple(VMEM for _ in outs),
        scratch_shapes=list(scratch),
        compiler_params=pltpu.CompilerParams(vmem_limit_bytes=mib << 20),
    )


def on_device(
    inv_sep,
    lower_one,
    upper_one,
    diag_inv_one,
    blocks_one,
    lower_two,
    upper_two,
    corner_lower,
    corner_upper,
    diag_inv_two,
    blocks_two,
):
    nr, nc = lax.axis_size("row"), lax.axis_size("col")
    nz = nc // 2
    blocks_one, blocks_two = in_hbm(blocks_one), in_hbm(blocks_two)
    rows_here, cols_here = inv_sep.shape
    width = diag_inv_one.shape[0]
    run_blocks = cols_here // B
    p1, p2 = blocks_one.shape[0] // nc, blocks_two.shape[0] // nc
    runs = nc // nr
    g1, g2 = p1 * runs, p2 * runs
    n1, n2 = p1 * B, p2 * B
    m1, m2 = g1 * B, g2 * B
    s1, s2 = m1 // nc, m2 // nc
    lw, uw, rw = width // nr, width // nc, width // nr
    unit = min(B, s2)

    def place_col(one, two, b):
        j = lax.axis_index("col")
        block = two[j * p2 + b]
        return sum((one[j * p1 + a] < block).astype(jnp.int32) for a in range(p1))

    def place_row(one, two, k):
        i = lax.axis_index("row")
        run = k // p2
        block = two[i * g2 + k]
        return run * p1 + sum((one[i * g1 + run * p1 + a] < block).astype(jnp.int32) for a in range(p1))

    def pick_panels(one, two, low1, low2, up1, up2, low, up, sems):
        i, j = lax.axis_index("row"), lax.axis_index("col")

        def lanes(block):
            return pl.ds(pl.multiple_of(block * B, B), B)

        for a in range(p1):
            pltpu.make_async_copy(
                low1.at[:, lanes(one[j * p1 + a] - j * run_blocks)], low.at[:, pl.ds(a * B, B)], sems.at[0]
            ).start()
        for a in range(p2):
            pltpu.make_async_copy(
                low2.at[:, lanes(two[j * p2 + a] - j * run_blocks)], low.at[:, pl.ds(n1 + a * B, B)], sems.at[0]
            ).start()
        for a in range(g1):
            pltpu.make_async_copy(
                up1.at[:, lanes(one[i * g1 + a] - i * (rows_here // B))], up.at[:, pl.ds(a * B, B)], sems.at[1]
            ).start()
        for a in range(g2):
            pltpu.make_async_copy(
                up2.at[:, lanes(two[i * g2 + a] - i * (rows_here // B))], up.at[:, pl.ds(m1 + a * B, B)], sems.at[1]
            ).start()
        pltpu.make_async_copy(low, low, sems.at[0]).wait()
        pltpu.make_async_copy(up, up, sems.at[1]).wait()

    low, up = call(
        pick_panels,
        [SMEM, SMEM, HBM, HBM, HBM, HBM],
        [shape((lw, n1 + n2), BF16), shape((uw, m1 + m2), BF16)],
        [pltpu.SemaphoreType.DMA((2,))],
    )(blocks_one, blocks_two, *map(in_hbm, (lower_one.T, lower_two.T, upper_one, upper_two)))

    ups = [up] + [exchange(up, "col", nc, 2 * k) for k in range(1, nz)]
    lows = [low] + [exchange(low, "row", nr, k) for k in range(1, nr)]
    others = [exchange(u, "col", nc, 1) for u in ups]

    def pick_sep(one, whole, d1, d2, cl, cu, sep, base, sem):
        i, j = lax.axis_index("row"), lax.axis_index("col")
        for a in range(g1):
            r = pl.multiple_of((one[i * g1 + a] - i * (rows_here // B)) * B, B)
            for b in range(p1):
                c = pl.multiple_of((one[j * p1 + b] - j * run_blocks) * B, B)
                pltpu.make_async_copy(
                    whole.at[pl.ds(r, B), pl.ds(c, B)], sep.at[pl.ds(a * B, B), pl.ds(b * B, B)], sem
                ).start()
        inner = jnp.dot(d1[...], cl[...].astype(F32), precision=lax.Precision.HIGHEST, preferred_element_type=F32)
        base[...] = d2[...] + jnp.dot(
            cu[...].astype(F32), inner, precision=lax.Precision.HIGHEST, preferred_element_type=F32
        )
        pltpu.make_async_copy(sep, sep, sem).wait()

    sep, base = call(
        pick_sep,
        [SMEM, HBM, VMEM, VMEM, VMEM, VMEM],
        [shape((m1, n1), BF16), shape((width, width), F32)],
        [pltpu.SemaphoreType.DMA],
    )(blocks_one, in_hbm(inv_sep), diag_inv_one, diag_inv_two, corner_lower, corner_upper)

    def lower_products(*refs):
        one, two = refs[:2]
        parts = refs[2 : 2 + nr]
        sep, cl, first_out, high_out, low_out, own, send, panel, ext, prod1, prod2 = refs[2 + nr :]
        i, j = lax.axis_index("row"), lax.axis_index("col")
        for k in range(nr):
            panel[pl.ds(pl.multiple_of((i ^ k) * lw, lw), lw), :] = parts[k][...].astype(F32)
        first = panel[:, :n1].astype(BF16)
        ext[...] = jnp.zeros_like(ext)
        for b in range(p2):
            spot = pl.multiple_of(place_col(one, two, b) * B, B)
            ext[:, pl.ds(spot, B)] = panel[:, n1 + b * B : n1 + (b + 1) * B]
        second = ext[...] - lax.dot_general(cl[...], first, TN, preferred_element_type=F32)
        high, low = split(second)
        first_out[...] = first
        high_out[...] = high
        low_out[...] = low
        s = sep[...]
        prod1[...] = lax.dot_general(s, first, NT, preferred_element_type=F32)
        prod2[...] = lax.dot_general(s, high, NT, preferred_element_type=F32) + lax.dot_general(
            s, low, NT, preferred_element_type=F32
        )
        for core in range(2):
            target = own if core == 0 else send
            for k in range(nz):
                owner = j ^ (2 * k + core)
                target[k, :s1, :] = prod1[pl.ds(pl.multiple_of(owner * s1, 16), s1), :].astype(target.dtype)
                for v in range(s2 // unit):
                    row = owner * s2 + v * unit
                    spot = place_row(one, two, row // B) * B + row % B
                    target[k, s1 + v * unit : s1 + (v + 1) * unit, :] = prod2[
                        pl.ds(pl.multiple_of(spot, unit), unit), :
                    ].astype(target.dtype)

    first_l, high_l, low_l, own, send = call(
        lower_products,
        [SMEM, SMEM] + [VMEM] * (nr + 2),
        [shape((width, n1), BF16)] * 3
        + [
            shape((nz, s1 + s2, width), F32),
            shape((nz, s1 + s2, width), PAIR_TYPE),
        ],
        [
            pltpu.VMEM((width, n1 + n2), F32),
            pltpu.VMEM((width, n1), F32),
            pltpu.VMEM((m1, width), F32),
            pltpu.VMEM((m1, width), F32),
        ],
        mib=32,
    )(blocks_one, blocks_two, *lows, sep, corner_lower)

    got = exchange(send, "col", nc, 1)

    def upper_products(*refs):
        one, two = refs[:2]
        parts = refs[2 : 2 + nc]
        cu, sep, mine = refs[2 + nc : 5 + nc]
        sends = refs[5 + nc : 4 + nc + nr]
        panel, ext, total = refs[4 + nc + nr :]
        i, j = lax.axis_index("row"), lax.axis_index("col")
        for k in range(nc):
            owner = j ^ (2 * (k % nz) + k // nz)
            panel[pl.ds(pl.multiple_of(owner * uw, uw), uw), :] = parts[k][...].astype(F32)
        ext[...] = jnp.zeros_like(ext)
        for b in range(g2):
            spot = pl.multiple_of(place_row(one, two, b) * B, B)
            ext[:, pl.ds(spot, B)] = panel[:, m1 + b * B : m1 + (b + 1) * B]
        first = panel[:, :m1].astype(BF16)
        high, low = split(ext[...] - dot(cu[...], first))
        s = sep[...]
        total[:, :n1] = dot(first, s)
        total[:, n1:] = dot(high, s) + dot(low, s)
        for k in range(nr):
            rows = pl.ds(pl.multiple_of((i ^ k) * rw, rw), rw)
            out = mine if k == 0 else sends[k - 1]
            out[...] = total[rows, :].astype(out.dtype)

    umine, *usends = call(
        upper_products,
        [SMEM, SMEM] + [VMEM] * (nc + 2),
        [shape((rw, 2 * n1), F32)] + [shape((rw, 2 * n1), ROW_TYPE)] * (nr - 1),
        [
            pltpu.VMEM((width, m1 + m2), F32),
            pltpu.VMEM((width, m1), F32),
            pltpu.VMEM((width, 2 * n1), F32),
        ],
        mib=32,
    )(blocks_one, blocks_two, *ups, *others, corner_upper, sep)
    upper_got = [exchange(x, "row", nr, k) for k, x in enumerate(usends, 1)]

    def lower_pair(own, got, mine, *sends):
        mine[...] = own[0] + got[0].astype(F32)
        for k in range(1, nz):
            sends[k - 1][...] = (own[k] + got[k].astype(F32)).astype(Z_TYPE)

    mine, *sends = call(
        lower_pair, [VMEM] * 2, [shape((s1 + s2, width), F32)] + [shape((s1 + s2, width), Z_TYPE)] * (nz - 1), mib=16
    )(own, got)
    lower_got = [exchange(x, "col", nc, 2 * k) for k, x in enumerate(sends, 1)]

    def upper_final(*refs):
        one, two, mine = refs[:3]
        got = refs[3 : 2 + nr]
        lp, lh, ll, out1, out2, keep, send, second, part = refs[2 + nr :]
        total = mine[...]
        for g in got:
            total = total + g[...].astype(F32)
        out1[...] = (-total[:, :n1]).astype(BF16)
        second[...] = -total[:, n1:]
        for b in range(p2):
            spot = pl.multiple_of(place_col(one, two, b) * B, B)
            out2[:, b * B : (b + 1) * B] = second[:, pl.ds(spot, B)].astype(BF16)

        def nt(a, b):
            return lax.dot_general(a, b, NT, preferred_element_type=F32)

        qh, ql = split(total[:, :n1])
        part[0] = nt(qh, lp[...]) + nt(ql, lp[...])
        qh, ql = split(total[:, n1:])
        part[1] = nt(qh, lh[...]) + nt(ql, lh[...]) + nt(qh, ll[...])
        core = lax.axis_index("col") % 2
        keep[...] = part[core]
        send[...] = part[1 - core].astype(DIAG_PAIR)

    inv_upper_one, inv_upper_two, dkeep, dsend = call(
        upper_final,
        [SMEM] * 2 + [VMEM] * (nr + 3),
        [
            shape((rw, n1), BF16),
            shape((rw, n2), BF16),
            shape((rw, width), F32),
            shape((rw, width), DIAG_PAIR),
        ],
        [pltpu.VMEM((rw, n1), F32), pltpu.VMEM((2, rw, width), F32)],
    )(blocks_one, blocks_two, umine, *upper_got, first_l, high_l, low_l)
    dgot = exchange(dsend, "col", nc, 1)

    def diag_pair(keep, got, out):
        out[...] = (keep[...] + got[...].astype(F32)).astype(out.dtype)

    (dpart,) = call(diag_pair, [VMEM] * 2, [shape((rw, width), DIAG_Z)])(dkeep, dgot)
    dz = [dpart] + [exchange(dpart, "col", nc, 2 * k) for k in range(1, nz)]

    def diag_z(*refs):
        parts, out, slots = refs[:nz], refs[nz], refs[nz + 1]
        chip = lax.axis_index("col") // 2
        for k in range(nz):
            slots[chip ^ k] = parts[k][...].astype(F32)
        total = slots[0]
        for k in range(1, nz):
            total = total + slots[k]
        out[...] = total.astype(out.dtype)

    (dsum,) = call(diag_z, [VMEM] * nz, [shape((rw, width), DIAG_OUT)], [pltpu.VMEM((nz, rw, width), F32)])(*dz)
    dall = [dsum] + [exchange(dsum, "row", nr, k) for k in range(1, nr)]
    dother = [exchange(x, "col", nc, 1) for x in dall]

    def lower_final(mine, *refs):
        got, (out1, out2) = refs[:-2], refs[-2:]
        total = mine[...]
        for g in got:
            total = total + g[...].astype(F32)
        out1[...] = (-total[:s1]).astype(BF16)
        out2[...] = (-total[s1:]).astype(BF16)

    inv_lower_one, inv_lower_two = call(
        lower_final, [VMEM] * nz, [shape((s1, width), BF16), shape((s2, width), BF16)]
    )(mine, *lower_got)

    def diag_final(*refs):
        parts, (d1, base, out1, out2) = refs[: 2 * nr], refs[2 * nr :]
        i, core = lax.axis_index("row"), lax.axis_index("col") % 2
        for side in range(2):
            for k in range(nr):
                rows = pl.ds(pl.multiple_of((i ^ k) * rw, rw), rw)
                piece = parts[side * nr + k][...].astype(F32)

                @pl.when((core ^ side) == 0)
                def _():
                    out1[rows, :] = d1[rows, :] + piece

                @pl.when((core ^ side) == 1)
                def _():
                    out2[rows, :] = base[rows, :] + piece

    inv_diag_one, inv_diag_two = call(
        diag_final, [VMEM] * (2 * nr + 2), [shape((width, width), F32)] * 2
    )(*dall, *dother, diag_inv_one, base)
    return (inv_lower_one, inv_upper_one, inv_diag_one, inv_lower_two, inv_upper_two, inv_diag_two)


def solution(mesh):
    return jax.shard_map(
        on_device,
        mesh=mesh,
        in_specs=(
            P("row", "col"),
            P("col", "row"),
            P("col", "row"),
            P(),
            P(),
            P("col", "row"),
            P("col", "row"),
            P(),
            P(),
            P(),
            P(),
        ),
        out_specs=(
            P(("row", "col"), None),
            P("row", "col"),
            P(),
            P(("row", "col"), None),
            P("row", "col"),
            P(),
        ),
        check_vma=False,
    )
```

time: 327 us -> 74 us (0.23)
  waiting for transfers between devices: 170 us -> 31.4 us
  blocking collectives: 53.1 us -> 0 us
  local copies, waits for them, and re-layouts: 46.8 us -> 0.02 us
  starting transfers between devices: 0.39 us -> 27.5 us
  other arithmetic: 24.2 us -> 0 us
  matrix products: 17 us -> 0 us
  Pallas kernels: 0 us -> 13.9 us
  between operations: 14.1 us -> 0.76 us
    psum x1 -> x0, waiting for transfers between devices: 134 us -> none  [on_device(): lax.psum((first_part, second_part + extra_part), ('row', 'col'))]
    all_gather x4 -> x0, blocking collectives: 53.1 us -> none  [the longest x1 17.9 us: on_device(): lax.all_gather(take_cols(upper_one, row_one), 'col', axis=0, tiled=True)]
    reduce_scatter x4 -> x0, waiting for transfers between devices: 36.7 us -> none  [the longest x1 20.1 us: on_device(): lax.psum_scatter(-(direct + shifted_part), 'row', scatter_dimension=0, ti...]
    ppermute x0 -> x28, waiting for transfers between devices: none -> 31.4 us  [exchange(): return lax.ppermute(x, axis, [(s, s ^ distance) for s in range(size)])]
    gather x11 -> x0, local copies, waits for them, and re-layouts: 29.7 us -> none  [the longest x4 16.4 us: take_rows(): jnp.take(shaped, blocks, axis=0)]
    ppermute x0 -> x28, starting transfers between devices: none -> 27.5 us  [exchange(): return lax.ppermute(x, axis, [(s, s ^ distance) for s in range(size)])]
    dot_general x15 -> x0, matrix products: 17 us -> none  [the longest x5 6.69 us: highest(): jnp.dot(first_mat.astype(jnp.float32), second_mat.astype(jnp.float32), pr...]
    select_n x13 -> x0, other arithmetic: 14.8 us -> none  [the longest x6 12.9 us: take_rows(): jnp.take(shaped, blocks, axis=0)]
  transfers between devices with their start and end apart: 5 -> 28, of which waited for: 3 -> 14; matrix products, arithmetic and copies ran while one was open for 14% -> 0% of each run, Pallas kernels for 0% -> 12%
where the time goes in v1:
time: 74 us; the launch traced here: 73.7 us
  waiting for transfers between devices  31.4 us (42%)
  starting transfers between devices  27.5 us (37%)
  Pallas kernels  13.9 us (19%)
  between operations  0.76 us (1%)
    ppermute x28, waiting for transfers between devices, exchange(): return lax.ppermute(x, axis, [(s, s ^ distance) for s in range(size)])  31.4 us
    ppermute x28, starting transfers between devices, exchange(): return lax.ppermute(x, axis, [(s, s ^ distance) for s in range(size)])  27.5 us
    pallas_call x1, Pallas kernels, on_device(): call(upper_products, [SMEM, SMEM] + [VMEM] * (nc + 2), [shape((rw, 2 * n1...  3.03 us
    pallas_call x1, Pallas kernels, on_device(): call(pick_sep, [SMEM, HBM, VMEM, VMEM, VMEM, VMEM], [shape((m1, n1), BF16...  2.86 us
    pallas_call x1, Pallas kernels, on_device(): call(lower_products, [SMEM, SMEM] + [VMEM] * (nr + 2), [shape((width, n1)...  2.74 us
    pallas_call x1, Pallas kernels, on_device(): call(upper_final, [SMEM] * 2 + [VMEM] * (nr + 3), [shape((rw, n1), BF16),...  1.8 us
    pallas_call x1, Pallas kernels, on_device(): call(pick_panels, [SMEM, SMEM, HBM, HBM, HBM, HBM], [shape((lw, n1 + n2),...  1.76 us
  transfers between devices with their start and end apart: 28, of which 14 were waited for; matrix products, arithmetic and copies ran while one was open for 0% of the time, Pallas kernels for 12%

profile of v1, /device:TPU:0, one launch (start us, length us, event | category | flops | bytes accessed | tf_op | source)
XLA Modules:
  0.0 73.7 jit_solution(10578219226891565098)
XLA Ops:
  0.7 1.8 %shard_map.154 = (bf16[64,1152]{1,0:T(8,128)(2,1)S(1)}, bf16[32,2304]{1,0:T(8,128)(2,1)S(1)}) custom-call(s32[40]{0:T(128)} %refs_0_.5, s32[32]{0:T(128)} %refs_1_.5, bf16[64,3072]{1,0:T(8,128)(2,1)} %bitcast.2, bf16[64,3072]{1,0:T(8,128)(2,1)} %bitcast.3, bf16[32,6144]{1,0:T(8,128)(2,1)} %up1.1, bf16[32,6144]{1,0:T(8,128)(2,1)} %up2.1), custom_call_target="tpu_custom_call" | custom-call | tf_op jit(solution)/shard_map/pallas_call | solution.py:124
  2.4 3.0 %collective-permute-start = (bf16[64,1152]{1,0:T(8,128)(2,1)S(1)}, bf16[64,1152]{1,0:T(8,128)(2,1)S(1)}, u32[]{:S(2)}, u32[]{:S(2)}) collective-permute-start(bf16[64,1152]{1,0:T(8,128)(2,1)S(1)} %get-tuple-element.31.refs_2_), channel_id=1, source_target_pairs={{0,8},{8,0},{16,24},{24,16},{1,9},{9,1},{17,25},{25,17},{2,10},{10... | collective-permute-start | bytes 442376 | tf_op jit(solution)/shard_map/ppermute | solution.py:33
  5.5 1.5 %collective-permute-start.1 = (bf16[64,1152]{1,0:T(8,128)(2,1)S(1)}, bf16[64,1152]{1,0:T(8,128)(2,1)S(1)}, u32[]{:S(2)}, u32[]{:S(2)}) collective-permute-start(bf16[64,1152]{1,0:T(8,128)(2,1)S(1)} %get-tuple-element.31.refs_2_), channel_id=1, source_target_pairs={{0,16},{8,24},{16,0},{24,8},{1,17},{9,25},{17,1},{25,9},{2,18},{10... | collective-permute-start | bytes 442376 | tf_op jit(solution)/shard_map/ppermute | solution.py:33
  7.0 0.0 collective-permute-start.2
  7.0 2.9 %shard_map.155 = (bf16[1280,640]{1,0:T(8,128)(2,1)S(1)}, f32[256,256]{1,0:T(8,128)S(1)}) custom-call(s32[40]{0:T(128)} %refs_0_.5, bf16[6144,3072]{1,0:T(8,128)(2,1)} %whole.1, f32[256,256]{1,0:T(8,128)S(1)} %copy-done, f32[256,256]{1,0:T(8,128)S(1)} %copy-done.3, bf16[256,256]{1,0:T(8,128)(2,1)S(1)} %copy-done.1, bf16[256,256]{1,0:T(8,128)(2,1)S(1)} %copy-done.2), custom_call_target="tpu_custom_call" | custom-call | tf_op jit(solution)/shard_map/pallas_call | solution.py:150
  9.9 0.0 collective-permute-done.refs_3_
  9.9 4.0 %collective-permute-done.1.refs_4_ = bf16[64,1152]{1,0:T(8,128)(2,1)S(1)} collective-permute-done((bf16[64,1152]{1,0:T(8,128)(2,1)S(1)}, bf16[64,1152]{1,0:T(8,128)(2,1)S(1)}, u32[]{:S(2)}, u32[]{:S(2)}) %collective-permute-start.1) | collective-permute-done | bytes 147488 | tf_op jit(solution)/shard_map/ppermute | solution.py:33
  13.9 0.0 collective-permute-done.2.refs_5_
  13.9 2.7 %shard_map.156 = (bf16[256,640]{1,0:T(8,128)(2,1)S(1)}, bf16[256,640]{1,0:T(8,128)(2,1)S(1)}, bf16[256,640]{1,0:T(8,128)(2,1)S(1)}, f32[4,288,256]{2,1,0:T(8,128)S(1)}, f32[4,288,256]{2,1,0:T(8,128)S(1)}) custom-call(s32[40]{0:T(128)} %refs_0_.5, s32[32]{0:T(128)} %refs_1_.5, bf16[64,1152]{1,0:T(8,128)(2,1)S(1)} %get-tuple-element.31.refs_2_, ...), custom_call_target="tpu_custom_call" | custom-call | tf_op jit(solution)/shard_map/pallas_call | solution.py:191
  16.7 0.1 collective-permute-start.3
  16.8 1.6 %collective-permute-start.7 = (bf16[32,2304]{1,0:T(8,128)(2,1)S(1)}, bf16[32,2304]{1,0:T(8,128)(2,1)S(1)}, u32[]{:S(2)}, u32[]{:S(2)}) collective-permute-start(bf16[32,2304]{1,0:T(8,128)(2,1)S(1)} %get-tuple-element.40.refs_2_), channel_id=1, source_target_pairs={{0,2},{1,3},{2,0},{3,1},{4,6},{5,7},{6,4},{7,5},{8,10},{9,11},{10,... | collective-permute-start | bytes 442376 | tf_op jit(solution)/shard_map/ppermute | solution.py:33
  18.4 2.6 %collective-permute-start.8 = (bf16[32,2304]{1,0:T(8,128)(2,1)S(1)}, bf16[32,2304]{1,0:T(8,128)(2,1)S(1)}, u32[]{:S(2)}, u32[]{:S(2)}) collective-permute-start(bf16[32,2304]{1,0:T(8,128)(2,1)S(1)} %get-tuple-element.40.refs_2_), channel_id=1, source_target_pairs={{0,4},{1,5},{2,6},{3,7},{4,0},{5,1},{6,2},{7,3},{8,12},{9,13},{10,... | collective-permute-start | bytes 442376 | tf_op jit(solution)/shard_map/ppermute | solution.py:33
  21.0 0.2 collective-permute-start.9
  21.2 0.0 collective-permute-start.10
  21.2 4.5 %collective-permute-done.7.refs_3_ = bf16[32,2304]{1,0:T(8,128)(2,1)S(1)} collective-permute-done((bf16[32,2304]{1,0:T(8,128)(2,1)S(1)}, bf16[32,2304]{1,0:T(8,128)(2,1)S(1)}, u32[]{:S(2)}, u32[]{:S(2)}) %collective-permute-start.7) | collective-permute-done | bytes 147488 | tf_op jit(solution)/shard_map/ppermute | solution.py:33
  25.7 6.7 %collective-permute-done.8.refs_4_ = bf16[32,2304]{1,0:T(8,128)(2,1)S(1)} collective-permute-done((bf16[32,2304]{1,0:T(8,128)(2,1)S(1)}, bf16[32,2304]{1,0:T(8,128)(2,1)S(1)}, u32[]{:S(2)}, u32[]{:S(2)}) %collective-permute-start.8) | collective-permute-done | bytes 147488 | tf_op jit(solution)/shard_map/ppermute | solution.py:33
  32.4 0.5 collective-permute-start.13
  32.9 0.9 %collective-permute-done.12.refs_8_ = bf16[32,2304]{1,0:T(8,128)(2,1)S(1)} collective-permute-done((bf16[32,2304]{1,0:T(8,128)(2,1)S(1)}, bf16[32,2304]{1,0:T(8,128)(2,1)S(1)}, u32[]{:S(2)}, u32[]{:S(2)}) %collective-permute-start.12) | collective-permute-done | bytes 147488 | tf_op jit(solution)/shard_map/ppermute | solution.py:33
  33.8 0.2 collective-permute-done.13.refs_9_
  34.0 3.0 %shard_map.159 = (f32[64,1280]{1,0:T(8,128)S(1)}, bf16[64,1280]{1,0:T(8,128)(2,1)S(1)}, bf16[64,1280]{1,0:T(8,128)(2,1)S(1)}, bf16[64,1280]{1,0:T(8,128)(2,1)S(1)}) custom-call(s32[40]{0:T(128)} %refs_0_.5, s32[32]{0:T(128)} %refs_1_.5, bf16[32,2304]{1,0:T(8,128)(2,1)S(1)} %get-tuple-element.40.refs_2_, bf16[32,2304]{1,0:T(8,128)(2,1)S(1)} %collective-permute-done.7.refs_3_, ...), custom_call_target="tpu_custom_call" | custom-call | tf_op jit(solution)/shard_map/pallas_call | solution.py:234
  37.0 1.3 %collective-permute-start.14 = (bf16[64,1280]{1,0:T(8,128)(2,1)S(1)}, bf16[64,1280]{1,0:T(8,128)(2,1)S(1)}, u32[]{:S(2)}, u32[]{:S(2)}) collective-permute-start(bf16[64,1280]{1,0:T(8,128)(2,1)S(1)} %get-tuple-element.42), channel_id=1, source_target_pairs={{0,8},{8,0},{16,24},{24,16},{1,9},{9,1},{17,25},{25,17},{2,10},{10... | collective-permute-start | bytes 491528 | tf_op jit(solution)/shard_map/ppermute | solution.py:33
  38.3 0.9 %collective-permute-start.15 = (bf16[64,1280]{1,0:T(8,128)(2,1)S(1)}, bf16[64,1280]{1,0:T(8,128)(2,1)S(1)}, u32[]{:S(2)}, u32[]{:S(2)}) collective-permute-start(bf16[64,1280]{1,0:T(8,128)(2,1)S(1)} %get-tuple-element.43), channel_id=1, source_target_pairs={{0,16},{8,24},{16,0},{24,8},{1,17},{9,25},{17,1},{25,9},{2,18},{10... | collective-permute-start | bytes 491528 | tf_op jit(solution)/shard_map/ppermute | solution.py:33
  39.2 1.4 %collective-permute-start.16 = (bf16[64,1280]{1,0:T(8,128)(2,1)S(1)}, bf16[64,1280]{1,0:T(8,128)(2,1)S(1)}, u32[]{:S(2)}, u32[]{:S(2)}) collective-permute-start(bf16[64,1280]{1,0:T(8,128)(2,1)S(1)} %get-tuple-element.44), channel_id=1, source_target_pairs={{0,24},{8,16},{16,8},{24,0},{1,25},{9,17},{17,9},{25,1},{2,26},{10... | collective-permute-start | bytes 491528 | tf_op jit(solution)/shard_map/ppermute | solution.py:33
  40.6 3.6 %collective-permute-done.14.refs_3_ = bf16[64,1280]{1,0:T(8,128)(2,1)S(1)} collective-permute-done((bf16[64,1280]{1,0:T(8,128)(2,1)S(1)}, bf16[64,1280]{1,0:T(8,128)(2,1)S(1)}, u32[]{:S(2)}, u32[]{:S(2)}) %collective-permute-start.14) | collective-permute-done | bytes 163872 | tf_op jit(solution)/shard_map/ppermute | solution.py:33
  44.1 2.2 %collective-permute-done.15.refs_4_ = bf16[64,1280]{1,0:T(8,128)(2,1)S(1)} collective-permute-done((bf16[64,1280]{1,0:T(8,128)(2,1)S(1)}, bf16[64,1280]{1,0:T(8,128)(2,1)S(1)}, u32[]{:S(2)}, u32[]{:S(2)}) %collective-permute-start.15) | collective-permute-done | bytes 163872 | tf_op jit(solution)/shard_map/ppermute | solution.py:33
  46.4 1.6 %collective-permute-done.16.refs_5_ = bf16[64,1280]{1,0:T(8,128)(2,1)S(1)} collective-permute-done((bf16[64,1280]{1,0:T(8,128)(2,1)S(1)}, bf16[64,1280]{1,0:T(8,128)(2,1)S(1)}, u32[]{:S(2)}, u32[]{:S(2)}) %collective-permute-start.16) | collective-permute-done | bytes 163872 | tf_op jit(solution)/shard_map/ppermute | solution.py:33
  48.0 1.8 %shard_map.160 = (bf16[64,640]{1,0:T(8,128)(2,1)}, bf16[64,512]{1,0:T(8,128)(2,1)}, f32[64,256]{1,0:T(8,128)S(1)}, f32[64,256]{1,0:T(8,128)S(1)}) custom-call(s32[40]{0:T(128)} %refs_0_.5, s32[32]{0:T(128)} %refs_1_.5, f32[64,1280]{1,0:T(8,128)S(1)} %get-tuple-element.41.refs_2_, bf16[64,1280]{1,0:T(8,128)(2,1)S(1)} %collective-permute-done.14.refs_3_, ...), custom_call_target="tpu_custom_call" | custom-call | tf_op jit(solution)/shard_map/pallas_call | solution.py:281
  49.8 1.3 %collective-permute-done.17.got = f32[64,256]{1,0:T(8,128)S(1)} collective-permute-done((f32[64,256]{1,0:T(8,128)S(1)}, f32[64,256]{1,0:T(8,128)S(1)}, u32[]{:S(2)}, u32[]{:S(2)}) %collective-permute-start.17) | collective-permute-done | bytes 65568 | tf_op jit(solution)/shard_map/ppermute | solution.py:33
  51.0 2.6 %collective-permute-start.18 = (bf16[64,256]{1,0:T(8,128)(2,1)S(1)}, bf16[64,256]{1,0:T(8,128)(2,1)S(1)}, u32[]{:S(2)}, u32[]{:S(2)}) collective-permute-start(bf16[64,256]{1,0:T(8,128)(2,1)S(1)} %shard_map.161.refs_0_), channel_id=1, source_target_pairs={{0,2},{1,3},{2,0},{3,1},{4,6},{5,7},{6,4},{7,5},{8,10},{9,11},{10,... | collective-permute-start | bytes 98312 | tf_op jit(solution)/shard_map/ppermute | solution.py:33
  53.6 1.1 %collective-permute-start.19 = (bf16[64,256]{1,0:T(8,128)(2,1)S(1)}, bf16[64,256]{1,0:T(8,128)(2,1)S(1)}, u32[]{:S(2)}, u32[]{:S(2)}) collective-permute-start(bf16[64,256]{1,0:T(8,128)(2,1)S(1)} %shard_map.161.refs_0_), channel_id=1, source_target_pairs={{0,4},{1,5},{2,6},{3,7},{4,0},{5,1},{6,2},{7,3},{8,12},{9,13},{10,... | collective-permute-start | bytes 98312 | tf_op jit(solution)/shard_map/ppermute | solution.py:33
  54.7 1.4 %collective-permute-start.20 = (bf16[64,256]{1,0:T(8,128)(2,1)S(1)}, bf16[64,256]{1,0:T(8,128)(2,1)S(1)}, u32[]{:S(2)}, u32[]{:S(2)}) collective-permute-start(bf16[64,256]{1,0:T(8,128)(2,1)S(1)} %shard_map.161.refs_0_), channel_id=1, source_target_pairs={{0,6},{1,7},{2,4},{3,5},{4,2},{5,3},{6,0},{7,1},{8,14},{9,15},{10,... | collective-permute-start | bytes 98312 | tf_op jit(solution)/shard_map/ppermute | solution.py:33
  56.1 0.1 shard_map.157
  56.2 1.1 %collective-permute-start.4 = (bf16[288,256]{1,0:T(8,128)(2,1)S(1)}, bf16[288,256]{1,0:T(8,128)(2,1)S(1)}, u32[]{:S(2)}, u32[]{:S(2)}) collective-permute-start(bf16[288,256]{1,0:T(8,128)(2,1)S(1)} %get-tuple-element.36), channel_id=1, source_target_pairs={{0,2},{1,3},{2,0},{3,1},{4,6},{5,7},{6,4},{7,5},{8,10},{9,11},{10,... | collective-permute-start | bytes 442376 | tf_op jit(solution)/shard_map/ppermute | solution.py:33
  57.3 2.0 %collective-permute-start.5 = (bf16[288,256]{1,0:T(8,128)(2,1)S(1)}, bf16[288,256]{1,0:T(8,128)(2,1)S(1)}, u32[]{:S(2)}, u32[]{:S(2)}) collective-permute-start(bf16[288,256]{1,0:T(8,128)(2,1)S(1)} %get-tuple-element.37), channel_id=1, source_target_pairs={{0,4},{1,5},{2,6},{3,7},{4,0},{5,1},{6,2},{7,3},{8,12},{9,13},{10,... | collective-permute-start | bytes 442376 | tf_op jit(solution)/shard_map/ppermute | solution.py:33
  59.3 1.4 %collective-permute-start.6 = (bf16[288,256]{1,0:T(8,128)(2,1)S(1)}, bf16[288,256]{1,0:T(8,128)(2,1)S(1)}, u32[]{:S(2)}, u32[]{:S(2)}) collective-permute-start(bf16[288,256]{1,0:T(8,128)(2,1)S(1)} %get-tuple-element.38), channel_id=1, source_target_pairs={{0,6},{1,7},{2,4},{3,5},{4,2},{5,3},{6,0},{7,1},{8,14},{9,15},{10,... | collective-permute-start | bytes 442376 | tf_op jit(solution)/shard_map/ppermute | solution.py:33
  60.7 0.1 collective-permute-done.20.refs_3_
  60.8 0.9 %collective-permute-start.21 = (bf16[64,256]{1,0:T(8,128)(2,1)S(1)}, bf16[64,256]{1,0:T(8,128)(2,1)S(1)}, u32[]{:S(2)}, u32[]{:S(2)}) collective-permute-start(bf16[64,256]{1,0:T(8,128)(2,1)S(1)} %shard_map.162.refs_0_), channel_id=1, source_target_pairs={{0,8},{8,0},{16,24},{24,16},{1,9},{9,1},{17,25},{25,17},{2,10},{10... | collective-permute-start | bytes 98312 | tf_op jit(solution)/shard_map/ppermute | solution.py:33
  61.7 1.5 %collective-permute-start.22 = (bf16[64,256]{1,0:T(8,128)(2,1)S(1)}, bf16[64,256]{1,0:T(8,128)(2,1)S(1)}, u32[]{:S(2)}, u32[]{:S(2)}) collective-permute-start(bf16[64,256]{1,0:T(8,128)(2,1)S(1)} %shard_map.162.refs_0_), channel_id=1, source_target_pairs={{0,16},{8,24},{16,0},{24,8},{1,17},{9,25},{17,1},{25,9},{2,18},{10... | collective-permute-start | bytes 98312 | tf_op jit(solution)/shard_map/ppermute | solution.py:33
  63.2 1.6 %collective-permute-done.21.refs_1_ = bf16[64,256]{1,0:T(8,128)(2,1)S(1)} collective-permute-done((bf16[64,256]{1,0:T(8,128)(2,1)S(1)}, bf16[64,256]{1,0:T(8,128)(2,1)S(1)}, u32[]{:S(2)}, u32[]{:S(2)}) %collective-permute-start.21) | collective-permute-done | bytes 32800 | tf_op jit(solution)/shard_map/ppermute | solution.py:33
  64.8 1.7 %collective-permute-start.23 = (bf16[64,256]{1,0:T(8,128)(2,1)S(1)}, bf16[64,256]{1,0:T(8,128)(2,1)S(1)}, u32[]{:S(2)}, u32[]{:S(2)}) collective-permute-start(bf16[64,256]{1,0:T(8,128)(2,1)S(1)} %shard_map.162.refs_0_), channel_id=1, source_target_pairs={{0,24},{8,16},{16,8},{24,0},{1,25},{9,17},{17,9},{25,1},{2,26},{10... | collective-permute-start | bytes 98312 | tf_op jit(solution)/shard_map/ppermute | solution.py:33
  66.6 3.1 %collective-permute-done.23.refs_3_ = bf16[64,256]{1,0:T(8,128)(2,1)S(1)} collective-permute-done((bf16[64,256]{1,0:T(8,128)(2,1)S(1)}, bf16[64,256]{1,0:T(8,128)(2,1)S(1)}, u32[]{:S(2)}, u32[]{:S(2)}) %collective-permute-start.23) | collective-permute-done | bytes 32800 | tf_op jit(solution)/shard_map/ppermute | solution.py:33
  69.6 0.5 collective-permute-start.26
  70.1 0.7 collective-permute-done.25.refs_5_
  70.8 0.2 collective-permute-start.27
  71.0 0.0 collective-permute-done.26.refs_6_
  71.0 1.0 %collective-permute-done.27.refs_7_ = bf16[64,256]{1,0:T(8,128)(2,1)S(1)} collective-permute-done((bf16[64,256]{1,0:T(8,128)(2,1)S(1)}, bf16[64,256]{1,0:T(8,128)(2,1)S(1)}, u32[]{:S(2)}, u32[]{:S(2)}) %collective-permute-start.27) | collective-permute-done | bytes 32800 | tf_op jit(solution)/shard_map/ppermute | solution.py:33
  72.0 0.9 %shard_map.163 = (f32[256,256]{1,0:T(8,128)}, f32[256,256]{1,0:T(8,128)}) custom-call(bf16[64,256]{1,0:T(8,128)(2,1)S(1)} %shard_map.162.refs_0_, bf16[64,256]{1,0:T(8,128)(2,1)S(1)} %collective-permute-done.21.refs_1_, bf16[64,256]{1,0:T(8,128)(2,1)S(1)} %collective-permute-done.22.refs_2_, bf16[64,256]{1,0:T(8,128)(2,1)S(1)} %collective-permute-done.23.refs_3_, ...), custom_call_target="tpu_custom_call" | custom-call | tf_op jit(solution)/shard_map/pallas_call | solution.py:342
  72.9 0.7 shard_map.158
  (26 shorter events, 0.1 us)
Async XLA Ops:
  0.6 6.4 %copy-start = (f32[256,256]{1,0:T(8,128)S(1)}, f32[256,256]{1,0:T(8,128)}, u32[]{:S(2)}) copy-start(f32[256,256]{1,0:T(8,128)} %refs_8_.1) | copy-start | bytes 786436
  0.6 6.4 %copy-start.3 = (f32[256,256]{1,0:T(8,128)S(1)}, f32[256,256]{1,0:T(8,128)}, u32[]{:S(2)}) copy-start(f32[256,256]{1,0:T(8,128)} %d2.1) | copy-start | bytes 786436
  0.7 6.4 %copy-start.1 = (bf16[256,256]{1,0:T(8,128)(2,1)S(1)}, bf16[256,256]{1,0:T(8,128)(2,1)}, u32[]{:S(2)}) copy-start(bf16[256,256]{1,0:T(8,128)(2,1)} %refs_7_.1) | copy-start | bytes 393220
  0.7 6.4 %copy-start.2 = (bf16[256,256]{1,0:T(8,128)(2,1)S(1)}, bf16[256,256]{1,0:T(8,128)(2,1)}, u32[]{:S(2)}) copy-start(bf16[256,256]{1,0:T(8,128)(2,1)} %refs_10_.1) | copy-start | bytes 393220
  2.4 7.5 %collective-permute-start = (bf16[64,1152]{1,0:T(8,128)(2,1)S(1)}, bf16[64,1152]{1,0:T(8,128)(2,1)S(1)}, u32[]{:S(2)}, u32[]{:S(2)}) collective-permute-start(bf16[64,1152]{1,0:T(8,128)(2,1)S(1)} %get-tuple-element.31.refs_2_), channel_id=1, source_target_pairs={{0,8},{8,0},{16,24},{24,16},{1,9},{9,1},{17,25},{25,17},{2,10},{10... | collective-permute-start | bytes 442376 | tf_op jit(solution)/shard_map/ppermute | solution.py:33
  5.5 8.5 %collective-permute-start.1 = (bf16[64,1152]{1,0:T(8,128)(2,1)S(1)}, bf16[64,1152]{1,0:T(8,128)(2,1)S(1)}, u32[]{:S(2)}, u32[]{:S(2)}) collective-permute-start(bf16[64,1152]{1,0:T(8,128)(2,1)S(1)} %get-tuple-element.31.refs_2_), channel_id=1, source_target_pairs={{0,16},{8,24},{16,0},{24,8},{1,17},{9,25},{17,1},{25,9},{2,18},{10... | collective-permute-start | bytes 442376 | tf_op jit(solution)/shard_map/ppermute | solution.py:33
  7.0 7.0 %collective-permute-start.2 = (bf16[64,1152]{1,0:T(8,128)(2,1)S(1)}, bf16[64,1152]{1,0:T(8,128)(2,1)S(1)}, u32[]{:S(2)}, u32[]{:S(2)}) collective-permute-start(bf16[64,1152]{1,0:T(8,128)(2,1)S(1)} %get-tuple-element.31.refs_2_), channel_id=1, source_target_pairs={{0,24},{8,16},{16,8},{24,0},{1,25},{9,17},{17,9},{25,1},{2,26},{10... | collective-permute-start | bytes 442376 | tf_op jit(solution)/shard_map/ppermute | solution.py:33
  16.7 39.4 %collective-permute-start.3 = (f32[4,288,256]{2,1,0:T(8,128)S(1)}, f32[4,288,256]{2,1,0:T(8,128)S(1)}, u32[]{:S(2)}, u32[]{:S(2)}) collective-permute-start(f32[4,288,256]{2,1,0:T(8,128)S(1)} %get-tuple-element.34), channel_id=1, source_target_pairs={{0,1},{1,0},{2,3},{3,2},{4,5},{5,4},{6,7},{7,6},{8,9},{9,8},{10,11... | collective-permute-start | bytes 3538952 | tf_op jit(solution)/shard_map/ppermute | solution.py:33
  16.8 8.9 %collective-permute-start.7 = (bf16[32,2304]{1,0:T(8,128)(2,1)S(1)}, bf16[32,2304]{1,0:T(8,128)(2,1)S(1)}, u32[]{:S(2)}, u32[]{:S(2)}) collective-permute-start(bf16[32,2304]{1,0:T(8,128)(2,1)S(1)} %get-tuple-element.40.refs_2_), channel_id=1, source_target_pairs={{0,2},{1,3},{2,0},{3,1},{4,6},{5,7},{6,4},{7,5},{8,10},{9,11},{10,... | collective-permute-start | bytes 442376 | tf_op jit(solution)/shard_map/ppermute | solution.py:33
  18.4 14.0 %collective-permute-start.8 = (bf16[32,2304]{1,0:T(8,128)(2,1)S(1)}, bf16[32,2304]{1,0:T(8,128)(2,1)S(1)}, u32[]{:S(2)}, u32[]{:S(2)}) collective-permute-start(bf16[32,2304]{1,0:T(8,128)(2,1)S(1)} %get-tuple-element.40.refs_2_), channel_id=1, source_target_pairs={{0,4},{1,5},{2,6},{3,7},{4,0},{5,1},{6,2},{7,3},{8,12},{9,13},{10,... | collective-permute-start | bytes 442376 | tf_op jit(solution)/shard_map/ppermute | solution.py:33
  21.0 11.4 %collective-permute-start.9 = (bf16[32,2304]{1,0:T(8,128)(2,1)S(1)}, bf16[32,2304]{1,0:T(8,128)(2,1)S(1)}, u32[]{:S(2)}, u32[]{:S(2)}) collective-permute-start(bf16[32,2304]{1,0:T(8,128)(2,1)S(1)} %get-tuple-element.40.refs_2_), channel_id=1, source_target_pairs={{0,6},{1,7},{2,4},{3,5},{4,2},{5,3},{6,0},{7,1},{8,14},{9,15},{10,... | collective-permute-start | bytes 442376 | tf_op jit(solution)/shard_map/ppermute | solution.py:33
  21.2 11.7 %collective-permute-start.10 = (bf16[32,2304]{1,0:T(8,128)(2,1)S(1)}, bf16[32,2304]{1,0:T(8,128)(2,1)S(1)}, u32[]{:S(2)}, u32[]{:S(2)}) collective-permute-start(bf16[32,2304]{1,0:T(8,128)(2,1)S(1)} %get-tuple-element.40.refs_2_), channel_id=1, source_target_pairs={{0,1},{1,0},{2,3},{3,2},{4,5},{5,4},{6,7},{7,6},{8,9},{9,8},{10,11... | collective-permute-start | bytes 442376 | tf_op jit(solution)/shard_map/ppermute | solution.py:33
  25.7 7.2 %collective-permute-start.11 = (bf16[32,2304]{1,0:T(8,128)(2,1)S(1)}, bf16[32,2304]{1,0:T(8,128)(2,1)S(1)}, u32[]{:S(2)}, u32[]{:S(2)}) collective-permute-start(bf16[32,2304]{1,0:T(8,128)(2,1)S(1)} %collective-permute-done.7.refs_3_), channel_id=1, source_target_pairs={{0,1},{1,0},{2,3},{3,2},{4,5},{5,4},{6,7},{7,6},{8,9},{9,8},{10,11... | collective-permute-start | bytes 442376 | tf_op jit(solution)/shard_map/ppermute | solution.py:33
  32.4 1.4 %collective-permute-start.12 = (bf16[32,2304]{1,0:T(8,128)(2,1)S(1)}, bf16[32,2304]{1,0:T(8,128)(2,1)S(1)}, u32[]{:S(2)}, u32[]{:S(2)}) collective-permute-start(bf16[32,2304]{1,0:T(8,128)(2,1)S(1)} %collective-permute-done.8.refs_4_), channel_id=1, source_target_pairs={{0,1},{1,0},{2,3},{3,2},{4,5},{5,4},{6,7},{7,6},{8,9},{9,8},{10,11... | collective-permute-start | bytes 442376 | tf_op jit(solution)/shard_map/ppermute | solution.py:33
  32.4 1.6 %collective-permute-start.13 = (bf16[32,2304]{1,0:T(8,128)(2,1)S(1)}, bf16[32,2304]{1,0:T(8,128)(2,1)S(1)}, u32[]{:S(2)}, u32[]{:S(2)}) collective-permute-start(bf16[32,2304]{1,0:T(8,128)(2,1)S(1)} %collective-permute-done.9.refs_5_), channel_id=1, source_target_pairs={{0,1},{1,0},{2,3},{3,2},{4,5},{5,4},{6,7},{7,6},{8,9},{9,8},{10,11... | collective-permute-start | bytes 442376 | tf_op jit(solution)/shard_map/ppermute | solution.py:33
  37.0 7.1 %collective-permute-start.14 = (bf16[64,1280]{1,0:T(8,128)(2,1)S(1)}, bf16[64,1280]{1,0:T(8,128)(2,1)S(1)}, u32[]{:S(2)}, u32[]{:S(2)}) collective-permute-start(bf16[64,1280]{1,0:T(8,128)(2,1)S(1)} %get-tuple-element.42), channel_id=1, source_target_pairs={{0,8},{8,0},{16,24},{24,16},{1,9},{9,1},{17,25},{25,17},{2,10},{10... | collective-permute-start | bytes 491528 | tf_op jit(solution)/shard_map/ppermute | solution.py:33
  38.3 8.1 %collective-permute-start.15 = (bf16[64,1280]{1,0:T(8,128)(2,1)S(1)}, bf16[64,1280]{1,0:T(8,128)(2,1)S(1)}, u32[]{:S(2)}, u32[]{:S(2)}) collective-permute-start(bf16[64,1280]{1,0:T(8,128)(2,1)S(1)} %get-tuple-element.43), channel_id=1, source_target_pairs={{0,16},{8,24},{16,0},{24,8},{1,17},{9,25},{17,1},{25,9},{2,18},{10... | collective-permute-start | bytes 491528 | tf_op jit(solution)/shard_map/ppermute | solution.py:33
  39.2 8.8 %collective-permute-start.16 = (bf16[64,1280]{1,0:T(8,128)(2,1)S(1)}, bf16[64,1280]{1,0:T(8,128)(2,1)S(1)}, u32[]{:S(2)}, u32[]{:S(2)}) collective-permute-start(bf16[64,1280]{1,0:T(8,128)(2,1)S(1)} %get-tuple-element.44), channel_id=1, source_target_pairs={{0,24},{8,16},{16,8},{24,0},{1,25},{9,17},{17,9},{25,1},{2,26},{10... | collective-permute-start | bytes 491528 | tf_op jit(solution)/shard_map/ppermute | solution.py:33
  49.8 1.3 %collective-permute-start.17 = (f32[64,256]{1,0:T(8,128)S(1)}, f32[64,256]{1,0:T(8,128)S(1)}, u32[]{:S(2)}, u32[]{:S(2)}) collective-permute-start(f32[64,256]{1,0:T(8,128)S(1)} %get-tuple-element.50), channel_id=1, source_target_pairs={{0,1},{1,0},{2,3},{3,2},{4,5},{5,4},{6,7},{7,6},{8,9},{9,8},{10,11... | collective-permute-start | bytes 196616 | tf_op jit(solution)/shard_map/ppermute | solution.py:33
  51.0 8.3 %collective-permute-start.18 = (bf16[64,256]{1,0:T(8,128)(2,1)S(1)}, bf16[64,256]{1,0:T(8,128)(2,1)S(1)}, u32[]{:S(2)}, u32[]{:S(2)}) collective-permute-start(bf16[64,256]{1,0:T(8,128)(2,1)S(1)} %shard_map.161.refs_0_), channel_id=1, source_target_pairs={{0,2},{1,3},{2,0},{3,1},{4,6},{5,7},{6,4},{7,5},{8,10},{9,11},{10,... | collective-permute-start | bytes 98312 | tf_op jit(solution)/shard_map/ppermute | solution.py:33
  53.6 7.1 %collective-permute-start.19 = (bf16[64,256]{1,0:T(8,128)(2,1)S(1)}, bf16[64,256]{1,0:T(8,128)(2,1)S(1)}, u32[]{:S(2)}, u32[]{:S(2)}) collective-permute-start(bf16[64,256]{1,0:T(8,128)(2,1)S(1)} %shard_map.161.refs_0_), channel_id=1, source_target_pairs={{0,4},{1,5},{2,6},{3,7},{4,0},{5,1},{6,2},{7,3},{8,12},{9,13},{10,... | collective-permute-start | bytes 98312 | tf_op jit(solution)/shard_map/ppermute | solution.py:33
  54.7 6.1 %collective-permute-start.20 = (bf16[64,256]{1,0:T(8,128)(2,1)S(1)}, bf16[64,256]{1,0:T(8,128)(2,1)S(1)}, u32[]{:S(2)}, u32[]{:S(2)}) collective-permute-start(bf16[64,256]{1,0:T(8,128)(2,1)S(1)} %shard_map.161.refs_0_), channel_id=1, source_target_pairs={{0,6},{1,7},{2,4},{3,5},{4,2},{5,3},{6,0},{7,1},{8,14},{9,15},{10,... | collective-permute-start | bytes 98312 | tf_op jit(solution)/shard_map/ppermute | solution.py:33
  56.2 16.7 %collective-permute-start.4 = (bf16[288,256]{1,0:T(8,128)(2,1)S(1)}, bf16[288,256]{1,0:T(8,128)(2,1)S(1)}, u32[]{:S(2)}, u32[]{:S(2)}) collective-permute-start(bf16[288,256]{1,0:T(8,128)(2,1)S(1)} %get-tuple-element.36), channel_id=1, source_target_pairs={{0,2},{1,3},{2,0},{3,1},{4,6},{5,7},{6,4},{7,5},{8,10},{9,11},{10,... | collective-permute-start | bytes 442376 | tf_op jit(solution)/shard_map/ppermute | solution.py:33
  57.3 15.6 %collective-permute-start.5 = (bf16[288,256]{1,0:T(8,128)(2,1)S(1)}, bf16[288,256]{1,0:T(8,128)(2,1)S(1)}, u32[]{:S(2)}, u32[]{:S(2)}) collective-permute-start(bf16[288,256]{1,0:T(8,128)(2,1)S(1)} %get-tuple-element.37), channel_id=1, source_target_pairs={{0,4},{1,5},{2,6},{3,7},{4,0},{5,1},{6,2},{7,3},{8,12},{9,13},{10,... | collective-permute-start | bytes 442376 | tf_op jit(solution)/shard_map/ppermute | solution.py:33
  59.3 13.6 %collective-permute-start.6 = (bf16[288,256]{1,0:T(8,128)(2,1)S(1)}, bf16[288,256]{1,0:T(8,128)(2,1)S(1)}, u32[]{:S(2)}, u32[]{:S(2)}) collective-permute-start(bf16[288,256]{1,0:T(8,128)(2,1)S(1)} %get-tuple-element.38), channel_id=1, source_target_pairs={{0,6},{1,7},{2,4},{3,5},{4,2},{5,3},{6,0},{7,1},{8,14},{9,15},{10,... | collective-permute-start | bytes 442376 | tf_op jit(solution)/shard_map/ppermute | solution.py:33
  60.8 4.0 %collective-permute-start.21 = (bf16[64,256]{1,0:T(8,128)(2,1)S(1)}, bf16[64,256]{1,0:T(8,128)(2,1)S(1)}, u32[]{:S(2)}, u32[]{:S(2)}) collective-permute-start(bf16[64,256]{1,0:T(8,128)(2,1)S(1)} %shard_map.162.refs_0_), channel_id=1, source_target_pairs={{0,8},{8,0},{16,24},{24,16},{1,9},{9,1},{17,25},{25,17},{2,10},{10... | collective-permute-start | bytes 98312 | tf_op jit(solution)/shard_map/ppermute | solution.py:33
  61.7 4.9 %collective-permute-start.22 = (bf16[64,256]{1,0:T(8,128)(2,1)S(1)}, bf16[64,256]{1,0:T(8,128)(2,1)S(1)}, u32[]{:S(2)}, u32[]{:S(2)}) collective-permute-start(bf16[64,256]{1,0:T(8,128)(2,1)S(1)} %shard_map.162.refs_0_), channel_id=1, source_target_pairs={{0,16},{8,24},{16,0},{24,8},{1,17},{9,25},{17,1},{25,9},{2,18},{10... | collective-permute-start | bytes 98312 | tf_op jit(solution)/shard_map/ppermute | solution.py:33
  64.8 4.8 %collective-permute-start.23 = (bf16[64,256]{1,0:T(8,128)(2,1)S(1)}, bf16[64,256]{1,0:T(8,128)(2,1)S(1)}, u32[]{:S(2)}, u32[]{:S(2)}) collective-permute-start(bf16[64,256]{1,0:T(8,128)(2,1)S(1)} %shard_map.162.refs_0_), channel_id=1, source_target_pairs={{0,24},{8,16},{16,8},{24,0},{1,25},{9,17},{17,9},{25,1},{2,26},{10... | collective-permute-start | bytes 98312 | tf_op jit(solution)/shard_map/ppermute | solution.py:33
  66.6 3.1 %collective-permute-start.24 = (bf16[64,256]{1,0:T(8,128)(2,1)S(1)}, bf16[64,256]{1,0:T(8,128)(2,1)S(1)}, u32[]{:S(2)}, u32[]{:S(2)}) collective-permute-start(bf16[64,256]{1,0:T(8,128)(2,1)S(1)} %shard_map.162.refs_0_), channel_id=1, source_target_pairs={{0,1},{1,0},{2,3},{3,2},{4,5},{5,4},{6,7},{7,6},{8,9},{9,8},{10,11... | collective-permute-start | bytes 98312 | tf_op jit(solution)/shard_map/ppermute | solution.py:33
  69.6 1.2 %collective-permute-start.25 = (bf16[64,256]{1,0:T(8,128)(2,1)S(1)}, bf16[64,256]{1,0:T(8,128)(2,1)S(1)}, u32[]{:S(2)}, u32[]{:S(2)}) collective-permute-start(bf16[64,256]{1,0:T(8,128)(2,1)S(1)} %collective-permute-done.21.refs_1_), channel_id=1, source_target_pairs={{0,1},{1,0},{2,3},{3,2},{4,5},{5,4},{6,7},{7,6},{8,9},{9,8},{10,11... | collective-permute-start | bytes 98312 | tf_op jit(solution)/shard_map/ppermute | solution.py:33
  69.6 1.4 %collective-permute-start.26 = (bf16[64,256]{1,0:T(8,128)(2,1)S(1)}, bf16[64,256]{1,0:T(8,128)(2,1)S(1)}, u32[]{:S(2)}, u32[]{:S(2)}) collective-permute-start(bf16[64,256]{1,0:T(8,128)(2,1)S(1)} %collective-permute-done.22.refs_2_), channel_id=1, source_target_pairs={{0,1},{1,0},{2,3},{3,2},{4,5},{5,4},{6,7},{7,6},{8,9},{9,8},{10,11... | collective-permute-start | bytes 98312 | tf_op jit(solution)/shard_map/ppermute | solution.py:33
  70.8 1.2 %collective-permute-start.27 = (bf16[64,256]{1,0:T(8,128)(2,1)S(1)}, bf16[64,256]{1,0:T(8,128)(2,1)S(1)}, u32[]{:S(2)}, u32[]{:S(2)}) collective-permute-start(bf16[64,256]{1,0:T(8,128)(2,1)S(1)} %collective-permute-done.23.refs_3_), channel_id=1, source_target_pairs={{0,1},{1,0},{2,3},{3,2},{4,5},{5,4},{6,7},{7,6},{8,9},{9,8},{10,11... | collective-permute-start | bytes 98312 | tf_op jit(solution)/shard_map/ppermute | solution.py:33
